TPU v7x, 32 devices: a whole 2x2x4 slice. The times are simulated.
32 devices in a mesh: rows: 8 (over z, y), cols: 4 (over x, core).
Axes of the slice: x: 2, y: 2, z: 4, core: 2. Of those that a mesh axis runs over, the one named last changes fastest.
Arguments:
- sketches: bfloat16 [2048, 16384], P('rows', 'cols'), may hold values from -6 to 6, as said below
- start_basis: bfloat16 [16384, 256], P('cols'), may hold values from -6 to 6
- shrink_index: int32 [1], replicated, may hold values from 64 to 191
Outputs:
- shrunk: float32 [256, 16384], P('rows', 'cols')
Inputs may be any that keep to these rules, and one draw needn't show every extreme that they name: `sketches`: real entries.
All inputs are finite; a program needn't handle non-finite values.
Results may differ from a plain program's by a relative error of at most 0.0028.
Values may be sent and summed in bfloat16 or wider, within the bound.
A program may use at most 64 MiB of HBM per device.

v0:
```python
import jax
import jax.numpy as jnp
from jax import lax
from jax.sharding import PartitionSpec as P

ITERS = 3
AXES = ("rows", "cols")
HIGHEST = lax.Precision.HIGHEST


def pieces(values):
    high = lax.reduce_precision(values, 8, 7)
    rest = values - high
    middle = lax.reduce_precision(rest, 8, 7)
    low = rest - middle
    return [part.astype(jnp.bfloat16) for part in (high, middle, low)]


def apply_sketches(strip, images):
    stacked = jnp.concatenate(pieces(images), axis=1)
    products = jnp.dot(strip, stacked, preferred_element_type=jnp.float32)
    high, middle, low = jnp.split(products, 3, axis=1)
    return high + (middle + low)


def all_sum(values):
    return lax.psum(values, AXES)


def inverse_factor(gram_total):
    lower_factor = jnp.linalg.cholesky(gram_total)
    identity = jnp.eye(gram_total.shape[0], dtype=jnp.float32)
    return jax.scipy.linalg.solve_triangular(lower_factor, identity, lower=True)


def body(sketches, start_basis, shrink_index):
    size = lax.axis_size("rows")
    strip = lax.all_to_all(sketches, "rows", split_axis=1, concat_axis=0, tiled=True)
    width = start_basis.shape[0] // size
    own_basis = lax.dynamic_slice_in_dim(start_basis, lax.axis_index("rows") * width, width, 0)
    projected = all_sum(jnp.dot(strip, own_basis, preferred_element_type=jnp.float32))
    for loop_index in range(ITERS):
        projected_bf = projected.astype(jnp.bfloat16)
        images = jnp.einsum("lw,lk->wk", strip, projected_bf, preferred_element_type=jnp.float32)
        raw = all_sum(apply_sketches(strip, images))
        gram_total = jnp.dot(projected_bf.astype(jnp.float32).T, raw, precision=HIGHEST)
        gram_total = 0.5 * (gram_total + gram_total.T)
        inverse = inverse_factor(gram_total)
        projected = jnp.dot(raw, inverse.T, precision=HIGHEST)
    energy = jnp.sum(projected * projected, axis=0)
    ordered = jnp.sort(energy)[::-1]
    threshold = lax.dynamic_index_in_dim(ordered, shrink_index[0], 0, keepdims=False)
    factor = jnp.sqrt(jnp.maximum(energy - threshold, 0.25 * threshold))
    scaled = jnp.dot(inverse * factor[:, None], images.T, precision=HIGHEST)
    return lax.all_to_all(scaled, "rows", split_axis=0, concat_axis=1, tiled=True)


def solution(mesh):
    return jax.shard_map(
        body,
        mesh=mesh,
        in_specs=(P("rows", "cols"), P("cols", None), P()),
        out_specs=P("rows", "cols"),
        check_vma=False,
    )
```

profile of v0, /device:TPU:0, one launch (start us, length us, event | category | flops | bytes accessed | tf_op | source)
XLA Modules:
  0.0 797.4 jit_solution(12065096326215861704)
XLA Ops:
  6.5 4.3 copy.18
  10.8 7.3 all-to-all-start
  18.1 48.3 %all-to-all-done = bf16[256,8,512]{0,2,1:T(8,128)(2,1)} async-done(((bf16[256,8,512]{0,2,1:T(8,128)(2,1)}), bf16[256,8,512]{0,2,1:T(8,128)(2,1)}, u32[]{:S(2)}, u32[]{:S(2)}) %all-to-all-start) | async-done | bytes 2097184 | tf_op jit(solution)/shard_map/all_to_all | solution.py:38
  74.0 59.7 %all-reduce.11 = bf16[2048,256]{0,1:T(8,128)(2,1)S(1)} all-reduce(f32[2048,256]{0,1:T(8,128)} %convolution_bitcast_fusion.3), channel_id=1, replica_groups=mesh['rows'=8,'cols'=4] {'rows','cols'}, use_global_device_ids=true, to_apply=%region_0.0 | all-reduce | flops 524288 | bytes 3145728 | tf_op jit(solution)/shard_map/psum | solution.py:27
  140.4 133.4 %all-reduce.6.cloned.1.call-done = f32[2048,256]{0,1:T(8,128)} async-done(((f32[2048,256]{0,1:T(8,128)}), f32[2048,256]{0,1:T(8,128)}) %all-reduce.6.cloned.1.call-update) | async-done | bytes 2097168 | tf_op jit(solution)/shard_map/psum | solution.py:27
  279.5 11.7 %cholesky.172 = f32[128,128]{1,0:T(8,128)S(1)} custom-call(f32[128,128]{1,0:T(8,128)S(1)} %cholesky.270), custom_call_target="Cholesky" | custom-call | tf_op jit(solution)/shard_map/jit(cholesky)/cholesky | solution.py:31
  291.2 9.8 %custom-call.15 = f32[1,128,128]{1,2,0:T(8,128)S(1)} custom-call(f32[1,128,128]{2,1,0:T(8,128)S(1)} %get-tuple-element.83), custom_call_target="InvertDiagBlocksLowerTriangular" | custom-call | tf_op jit(solution)/shard_map/jit(cholesky)/cholesky | solution.py:31
  301.5 11.7 %cholesky.189 = f32[128,128]{1,0:T(8,128)S(1)} custom-call(f32[128,128]{1,0:T(8,128)S(1)} %convolution_subtract_fusion.5), custom_call_target="Cholesky" | custom-call | tf_op jit(solution)/shard_map/jit(cholesky)/cholesky | solution.py:31
  315.3 4.5 while.6
  319.8 19.7 %custom-call.16 = f32[2,128,128]{1,2,0:T(8,128)S(1)} custom-call(f32[2,128,128]{2,1,0:T(8,128)S(1)} %get-tuple-element.30), custom_call_target="InvertDiagBlocksLowerTriangular" | custom-call | tf_op jit(solution)/shard_map/jit(_solve_triangular)/triangular_solve | solution.py:33
  340.4 5.1 convolution_convert_fusion.1
  350.2 133.4 %all-reduce.8.cloned.1.call-done = f32[2048,256]{0,1:T(8,128)} async-done(((f32[2048,256]{0,1:T(8,128)}), f32[2048,256]{0,1:T(8,128)}) %all-reduce.8.cloned.1.call-update) | async-done | bytes 2097168 | tf_op jit(solution)/shard_map/psum | solution.py:27
  489.5 11.7 %cholesky.206 = f32[128,128]{1,0:T(8,128)S(1)} custom-call(f32[128,128]{1,0:T(8,128)S(1)} %cholesky.273), custom_call_target="Cholesky" | custom-call | tf_op jit(solution)/shard_map/jit(cholesky)/cholesky | solution.py:31
  501.3 9.8 %custom-call.17 = f32[1,128,128]{1,2,0:T(8,128)S(1)} custom-call(f32[1,128,128]{2,1,0:T(8,128)S(1)} %get-tuple-element.79), custom_call_target="InvertDiagBlocksLowerTriangular" | custom-call | tf_op jit(solution)/shard_map/jit(cholesky)/cholesky | solution.py:31
  511.6 11.7 %cholesky.223 = f32[128,128]{1,0:T(8,128)S(1)} custom-call(f32[128,128]{1,0:T(8,128)S(1)} %convolution_subtract_fusion.4), custom_call_target="Cholesky" | custom-call | tf_op jit(solution)/shard_map/jit(cholesky)/cholesky | solution.py:31
  529.9 19.9 %custom-call.18 = f32[2,128,128]{1,2,0:T(8,128)S(1)} custom-call(f32[2,128,128]{2,1,0:T(8,128)S(1)} %get-tuple-element.31), custom_call_target="InvertDiagBlocksLowerTriangular" | custom-call | tf_op jit(solution)/shard_map/jit(_solve_triangular)/triangular_solve | solution.py:33
  550.7 5.1 convolution_convert_fusion
  561.7 132.9 %all-reduce.10.cloned.1.call-done = f32[2048,256]{0,1:T(8,128)} async-done(((f32[2048,256]{0,1:T(8,128)}), f32[2048,256]{0,1:T(8,128)}) %all-reduce.10.cloned.1.call-update) | async-done | bytes 2097168 | tf_op jit(solution)/shard_map/psum | solution.py:27
  700.6 11.7 %cholesky.240 = f32[128,128]{1,0:T(8,128)S(1)} custom-call(f32[128,128]{1,0:T(8,128)S(1)} %cholesky.276), custom_call_target="Cholesky" | custom-call | tf_op jit(solution)/shard_map/jit(cholesky)/cholesky | solution.py:31
  712.3 10.2 %custom-call.19 = f32[1,128,128]{1,2,0:T(8,128)S(1)} custom-call(f32[1,128,128]{2,1,0:T(8,128)S(1)} %get-tuple-element.75), custom_call_target="InvertDiagBlocksLowerTriangular" | custom-call | tf_op jit(solution)/shard_map/jit(cholesky)/cholesky | solution.py:31
  723.0 11.7 %cholesky.257 = f32[128,128]{1,0:T(8,128)S(1)} custom-call(f32[128,128]{1,0:T(8,128)S(1)} %convolution_subtract_fusion.3), custom_call_target="Cholesky" | custom-call | tf_op jit(solution)/shard_map/jit(cholesky)/cholesky | solution.py:31
  741.3 19.8 %custom-call.20 = f32[2,128,128]{1,2,0:T(8,128)S(1)} custom-call(f32[2,128,128]{2,1,0:T(8,128)S(1)} %get-tuple-element.32), custom_call_target="InvertDiagBlocksLowerTriangular" | custom-call | tf_op jit(solution)/shard_map/jit(_solve_triangular)/triangular_solve | solution.py:33
  762.0 5.0 fusion.3
  773.2 16.7 %all_to_all.38 = f32[8,32,512]{2,1,0:T(8,128)S(1)} all-to-all(f32[8,32,512]{2,1,0:T(8,128)S(1)} %bitcast.164), channel_id=1, replica_groups=mesh['rows'=8,'cols'=4] {'rows'}, dimensions={0} | all-to-all | bytes 1048576 | tf_op jit(solution)/shard_map/all_to_all | solution.py:55
  (110 shorter events, 75.1 us)
Async XLA Ops:
  6.5 63.8 %copy-start = (bf16[4096,256]{1,0:T(8,128)(2,1)S(1)}, bf16[4096,256]{1,0:T(8,128)(2,1)}, u32[]{:S(2)}) copy-start(bf16[4096,256]{1,0:T(8,128)(2,1)} %param.7) | copy-start | bytes 6291460
  10.8 55.7 %all-to-all-start = ((bf16[256,8,512]{0,2,1:T(8,128)(2,1)}), bf16[256,8,512]{0,2,1:T(8,128)(2,1)}, u32[]{:S(2)}, u32[]{:S(2)}) async-start(bf16[256,8,512]{0,2,1:T(8,128)(2,1)} %bitcast.163), calls=%async_computation | async-start | bytes 4194304 | tf_op jit(solution)/shard_map/all_to_all | solution.py:38
  18.1 255.6 %all-reduce.6.cloned.1.call-start = ((), (), s32[]{:S(2)}) async-start(), calls=%async_computation.2 | async-start | bytes 4194304 | tf_op jit(solution)/shard_map/psum | solution.py:27
  133.8 2.5 copy-start.1
  140.0 343.6 %all-reduce.8.cloned.1.call-start = ((), (), s32[]{:S(2)}) async-start(), calls=%async_computation.3 | async-start | bytes 4194304 | tf_op jit(solution)/shard_map/psum | solution.py:27
  339.8 5.7 copy-start.2
  350.0 344.6 %all-reduce.10.cloned.1.call-start = ((), (), s32[]{:S(2)}) async-start(), calls=%async_computation.4 | async-start | bytes 4194304 | tf_op jit(solution)/shard_map/psum | solution.py:27
  550.1 5.7 copy-start.3
  737.4 35.2 %copy-start.4 = (f32[256,512]{1,0:T(8,128)S(1)}, f32[256,512]{1,0:T(8,128)}, u32[]{:S(2)}) copy-start(f32[256,512]{1,0:T(8,128)} %get-tuple-element.88) | copy-start | bytes 1572868
Sparse Core Ops, SparseCore 0:
  140.1 133.5 all-reduce.5
  350.1 133.4 all-reduce.7
  561.1 133.3 all-reduce.9
where the time goes:
time: 802 us; the launch traced here: 797 us
  waiting for transfers between devices  448 us (56%)
  other arithmetic  176 us (22%)
  blocking collectives  76.4 us (10%)
  matrix products  44.7 us (6%)
  local copies, waits for them, and re-layouts  25.2 us (3%)
  between operations  18.9 us (2%)
    psum x3, waiting for transfers between devices, all_sum(): return lax.psum(values, AXES)  400 us
    another operation x20, other arithmetic, inverse_factor(): lower_factor = jnp.linalg.cholesky(gram_total)  104 us
    psum x1, blocking collectives, all_sum(): return lax.psum(values, AXES)  59.7 us
    another operation x7, other arithmetic, inverse_factor(): return jax.scipy.linalg.solve_triangular(lower_factor, identity, lower=True)  59.5 us
    all_to_all x1, waiting for transfers between devices, body(): lax.all_to_all(sketches, 'rows', split_axis=1, concat_axis=0, tiled=True)  48.3 us
    all_to_all x1, blocking collectives, body(): lax.all_to_all(scaled, 'rows', split_axis=0, concat_axis=1, tiled=True)  16.7 us
  transfers between devices with their start and end apart: 4, of which 4 were waited for; matrix products, arithmetic and copies ran while one was open for 0% of the time, Pallas kernels for 0%

commit v1 on v0

--- a/solution.py
+++ b/solution.py
@@ -35,7 +35,10 @@
 
 def body(sketches, start_basis, shrink_index):
     size = lax.axis_size("rows")
-    strip = lax.all_to_all(sketches, "rows", split_axis=1, concat_axis=0, tiled=True)
+    strip = jnp.concatenate(
+        lax.all_to_all(jnp.stack(jnp.split(sketches, lax.axis_size("rows"), axis=1)), "rows", 0, 0),
+        axis=0,
+    )
     width = start_basis.shape[0] // size
     own_basis = lax.dynamic_slice_in_dim(start_basis, lax.axis_index("rows") * width, width, 0)
     projected = all_sum(jnp.dot(strip, own_basis, preferred_element_type=jnp.float32))

time: 802 us -> 811 us (1.011)
  no operation moved by 1% of the time
where the time goes in v1:
time: 811 us; the launch traced here: 806 us
  waiting for transfers between devices  448 us (55%)
  other arithmetic  175 us (22%)
  blocking collectives  76.4 us (9%)
  matrix products  48.1 us (6%)
  local copies, waits for them, and re-layouts  30.6 us (4%)
  between operations  18.9 us (2%)
    psum x3, waiting for transfers between devices, all_sum(): return lax.psum(values, AXES)  400 us
    another operation x20, other arithmetic, inverse_factor(): lower_factor = jnp.linalg.cholesky(gram_total)  103 us
    psum x1, blocking collectives, all_sum(): return lax.psum(values, AXES)  59.7 us
    another operation x7, other arithmetic, inverse_factor(): return jax.scipy.linalg.solve_triangular(lower_factor, identity, lower=True)  59.5 us
    all_to_all x1, waiting for transfers between devices, body(): lax.all_to_all(jnp.stack(jnp.split(sketches, lax.axis_size('rows'), axis=...  48.3 us
    all_to_all x1, blocking collectives, body(): lax.all_to_all(scaled, 'rows', split_axis=0, concat_axis=1, tiled=True)  16.7 us
  transfers between devices with their start and end apart: 4, of which 4 were waited for; matrix products, arithmetic and copies ran while one was open for 0% of the time, Pallas kernels for 0%

profile of v1, /device:TPU:0, one launch (start us, length us, event | category | flops | bytes accessed | tf_op | source)
XLA Modules:
  0.0 805.6 jit_solution(9574993742333280356)
XLA Ops:
  20.1 7.3 all-to-all-start
  27.5 48.3 %all-to-all-done = bf16[8,256,512]{2,1,0:T(8,128)(2,1)} async-done(((bf16[8,256,512]{2,1,0:T(8,128)(2,1)}), bf16[8,256,512]{2,1,0:T(8,128)(2,1)}, u32[]{:S(2)}, u32[]{:S(2)}) %all-to-all-start) | async-done | bytes 2097184 | tf_op jit(solution)/shard_map/all_to_all | solution.py:39
  79.4 59.7 %all-reduce.11 = bf16[2048,256]{1,0:T(8,128)(2,1)S(1)} all-reduce(f32[2048,256]{1,0:T(8,128)} %fusion.43), channel_id=1, replica_groups=mesh['rows'=8,'cols'=4] {'rows','cols'}, use_global_device_ids=true, to_apply=%region_0.0 | all-reduce | flops 524288 | bytes 3145728 | tf_op jit(solution)/shard_map/psum | solution.py:27
  147.0 133.4 %all-reduce.6.cloned.1.call-done = f32[2048,256]{1,0:T(8,128)} async-done(((f32[2048,256]{1,0:T(8,128)}), f32[2048,256]{1,0:T(8,128)}) %all-reduce.6.cloned.1.call-update) | async-done | bytes 2097168 | tf_op jit(solution)/shard_map/psum | solution.py:27
  286.5 11.7 %cholesky.172 = f32[128,128]{1,0:T(8,128)S(1)} custom-call(f32[128,128]{1,0:T(8,128)S(1)} %cholesky.270), custom_call_target="Cholesky" | custom-call | tf_op jit(solution)/shard_map/jit(cholesky)/cholesky | solution.py:31
  298.3 9.8 %custom-call.15 = f32[1,128,128]{1,2,0:T(8,128)S(1)} custom-call(f32[1,128,128]{2,1,0:T(8,128)S(1)} %get-tuple-element.83), custom_call_target="InvertDiagBlocksLowerTriangular" | custom-call | tf_op jit(solution)/shard_map/jit(cholesky)/cholesky | solution.py:31
  308.5 11.7 %cholesky.189 = f32[128,128]{1,0:T(8,128)S(1)} custom-call(f32[128,128]{1,0:T(8,128)S(1)} %convolution_subtract_fusion.5), custom_call_target="Cholesky" | custom-call | tf_op jit(solution)/shard_map/jit(cholesky)/cholesky | solution.py:31
  322.3 4.5 while.6
  326.8 19.7 %custom-call.16 = f32[2,128,128]{1,2,0:T(8,128)S(1)} custom-call(f32[2,128,128]{2,1,0:T(8,128)S(1)} %get-tuple-element.30), custom_call_target="InvertDiagBlocksLowerTriangular" | custom-call | tf_op jit(solution)/shard_map/jit(_solve_triangular)/triangular_solve | solution.py:33
  358.6 133.4 %all-reduce.8.cloned.1.call-done = f32[2048,256]{1,0:T(8,128)} async-done(((f32[2048,256]{1,0:T(8,128)}), f32[2048,256]{1,0:T(8,128)}) %all-reduce.8.cloned.1.call-update) | async-done | bytes 2097168 | tf_op jit(solution)/shard_map/psum | solution.py:27
  492.1 3.8 fusion.87
  498.1 11.7 %cholesky.206 = f32[128,128]{1,0:T(8,128)S(1)} custom-call(f32[128,128]{1,0:T(8,128)S(1)} %cholesky.273), custom_call_target="Cholesky" | custom-call | tf_op jit(solution)/shard_map/jit(cholesky)/cholesky | solution.py:31
  509.9 9.8 %custom-call.17 = f32[1,128,128]{1,2,0:T(8,128)S(1)} custom-call(f32[1,128,128]{2,1,0:T(8,128)S(1)} %get-tuple-element.79), custom_call_target="InvertDiagBlocksLowerTriangular" | custom-call | tf_op jit(solution)/shard_map/jit(cholesky)/cholesky | solution.py:31
  520.2 11.7 %cholesky.223 = f32[128,128]{1,0:T(8,128)S(1)} custom-call(f32[128,128]{1,0:T(8,128)S(1)} %convolution_subtract_fusion.4), custom_call_target="Cholesky" | custom-call | tf_op jit(solution)/shard_map/jit(cholesky)/cholesky | solution.py:31
  534.6 3.9 while.7
  538.5 20.1 %custom-call.18 = f32[2,128,128]{1,2,0:T(8,128)S(1)} custom-call(f32[2,128,128]{2,1,0:T(8,128)S(1)} %get-tuple-element.31), custom_call_target="InvertDiagBlocksLowerTriangular" | custom-call | tf_op jit(solution)/shard_map/jit(_solve_triangular)/triangular_solve | solution.py:33
  571.9 132.8 %all-reduce.10.cloned.1.call-done = f32[2048,256]{1,0:T(8,128)} async-done(((f32[2048,256]{1,0:T(8,128)}), f32[2048,256]{1,0:T(8,128)}) %all-reduce.10.cloned.1.call-update) | async-done | bytes 2097168 | tf_op jit(solution)/shard_map/psum | solution.py:27
  704.7 3.8 fusion.88
  710.8 11.7 %cholesky.240 = f32[128,128]{1,0:T(8,128)S(1)} custom-call(f32[128,128]{1,0:T(8,128)S(1)} %cholesky.276), custom_call_target="Cholesky" | custom-call | tf_op jit(solution)/shard_map/jit(cholesky)/cholesky | solution.py:31
  722.6 9.9 %custom-call.19 = f32[1,128,128]{1,2,0:T(8,128)S(1)} custom-call(f32[1,128,128]{2,1,0:T(8,128)S(1)} %get-tuple-element.75), custom_call_target="InvertDiagBlocksLowerTriangular" | custom-call | tf_op jit(solution)/shard_map/jit(cholesky)/cholesky | solution.py:31
  733.0 11.7 %cholesky.257 = f32[128,128]{1,0:T(8,128)S(1)} custom-call(f32[128,128]{1,0:T(8,128)S(1)} %convolution_subtract_fusion.3), custom_call_target="Cholesky" | custom-call | tf_op jit(solution)/shard_map/jit(cholesky)/cholesky | solution.py:31
  747.4 3.9 while.8
  751.2 19.7 %custom-call.20 = f32[2,128,128]{1,2,0:T(8,128)S(1)} custom-call(f32[2,128,128]{2,1,0:T(8,128)S(1)} %get-tuple-element.32), custom_call_target="InvertDiagBlocksLowerTriangular" | custom-call | tf_op jit(solution)/shard_map/jit(_solve_triangular)/triangular_solve | solution.py:33
  781.4 16.7 %all_to_all.24 = f32[8,32,512]{2,1,0:T(8,128)S(1)} all-to-all(f32[8,32,512]{2,1,0:T(8,128)S(1)} %bitcast.151), channel_id=1, replica_groups=mesh['rows'=8,'cols'=4] {'rows'}, dimensions={0} | all-to-all | bytes 1048576 | tf_op jit(solution)/shard_map/all_to_all | solution.py:58
  (110 shorter events, 87.5 us)
Async XLA Ops:
  6.5 69.2 %copy-start = (bf16[4096,256]{1,0:T(8,128)(2,1)S(1)}, bf16[4096,256]{1,0:T(8,128)(2,1)}, u32[]{:S(2)}) copy-start(bf16[4096,256]{1,0:T(8,128)(2,1)} %param.7) | copy-start | bytes 6291460
  20.1 55.7 %all-to-all-start = ((bf16[8,256,512]{2,1,0:T(8,128)(2,1)}), bf16[8,256,512]{2,1,0:T(8,128)(2,1)}, u32[]{:S(2)}, u32[]{:S(2)}) async-start(bf16[8,256,512]{2,1,0:T(8,128)(2,1)} %bitcast_dynamic-update-slice_fusion.3), calls=%async_computation | async-start | bytes 4194304 | tf_op jit(solution)/shard_map/all_to_all | solution.py:39
  27.4 253.0 %all-reduce.6.cloned.1.call-start = ((), (), s32[]{:S(2)}) async-start(), calls=%async_computation.2 | async-start | bytes 4194304 | tf_op jit(solution)/shard_map/psum | solution.py:27
  146.7 345.4 %all-reduce.8.cloned.1.call-start = ((), (), s32[]{:S(2)}) async-start(), calls=%async_computation.3 | async-start | bytes 4194304 | tf_op jit(solution)/shard_map/psum | solution.py:27
  358.4 346.3 %all-reduce.10.cloned.1.call-start = ((), (), s32[]{:S(2)}) async-start(), calls=%async_computation.4 | async-start | bytes 4194304 | tf_op jit(solution)/shard_map/psum | solution.py:27
  747.3 33.4 %copy-start.1 = (f32[512,256]{0,1:T(8,128)S(1)}, f32[512,256]{0,1:T(8,128)}, u32[]{:S(2)}) copy-start(f32[512,256]{0,1:T(8,128)} %get-tuple-element.88) | copy-start | bytes 1572868
Sparse Core Ops, SparseCore 0:
  146.8 133.6 all-reduce.5
  358.5 133.5 all-reduce.7
  571.4 133.3 all-reduce.9
